TPU v7x, 256 devices: a whole 4x4x8 slice. The times are simulated.
256 devices in a mesh: view: 16 (over z, core), blk: 16 (over y, x).
Axes of the slice: x: 4, y: 4, z: 8, core: 2. Of those that a mesh axis runs over, the one named last changes fastest.
Arguments:
- estimate: float32 [256, 128, 128], P('blk'), may hold values from 0.5 to 2
- images: bfloat16 [16, 256, 64, 128], P('view', 'blk'), may hold values from 0.5 to 2
- point_spread: float32 [8, 9, 7, 25], replicated, may hold values from 0.01 to 1
- covered: int32 [8, 16, 4], P(None, 'blk'), may hold values from 0 to 1, as said below
Outputs:
- estimate_next: float32 [256, 128, 128], P('blk')
Inputs may be any that keep to these rules, and one draw needn't show every extreme that they name: For each view and each block layer along the first dimension, the covered blocks are consecutive along the second dimension and at most 3; for every view some block layer has exactly 3.
All inputs are finite; a program needn't handle non-finite values.
Results may differ from a plain program's by a relative error of at most 0.0003.
Values may be sent and summed in bfloat16 or wider, within the bound.
A program may use at most 64 MiB of HBM per device.

v0:
```python
import jax
import jax.numpy as jnp
from jax import lax
from jax.sharding import PartitionSpec as P

BY = 32


def with_halo(cells, sides, width):
    for axis, dim in sides:
        count = lax.axis_size(axis)
        ends = count - 1
        head = lax.slice_in_dim(cells, 0, width, axis=dim)
        tail = lax.slice_in_dim(cells, cells.shape[dim] - width, cells.shape[dim], axis=dim)
        cells = jnp.concatenate(
            [
                lax.ppermute(tail, axis, [(i, (i + 1) % count) for i in range(ends)]),
                cells,
                lax.ppermute(head, axis, [((i + 1) % count, i) for i in range(ends)]),
            ],
            axis=dim,
        )
    return cells


def swapped(block, axis, stride):
    count = lax.axis_size(axis)
    route = []
    for low in range(count):
        high = low | 1 << stride
        if high != low and high < count:
            route += [(low, high), (high, low)]
    return lax.ppermute(block, axis, route)


def merged(part, axis, combine):
    gathered = lax.all_gather(part, axis)

    def take(source):
        return lax.dynamic_index_in_dim(gathered, source, 0, False)

    return lax.fori_loop(
        1, lax.axis_size(axis), lambda source, state: combine(state, take(source)), take(0)
    )


def band_table(kernel, depth):
    taps_x, taps_y, taps_z = kernel.shape
    rim_z = (taps_z - 1) // 2
    shape_three = (taps_z, depth, depth)
    offset = lax.broadcasted_iota(jnp.int32, shape_three, 1) - lax.broadcasted_iota(
        jnp.int32, shape_three, 2
    )
    onehot = (offset + rim_z == lax.broadcasted_iota(jnp.int32, shape_three, 0)).astype(
        jnp.bfloat16
    )
    banded = jnp.einsum("abt,tpz->abpz", kernel, onehot, preferred_element_type=jnp.float32).astype(
        jnp.bfloat16
    )
    return banded.reshape(taps_x, taps_y * depth, depth)


def convolve(padded_part, banded, rows_x, rows_y):
    taps_x = padded_part.shape[0] - rows_x + 1
    taps_y = padded_part.shape[1] - rows_y + 1
    columns = jnp.concatenate(
        [padded_part[:, step_y : step_y + rows_y, :] for step_y in range(taps_y)], axis=2
    )
    output = None
    for shift_x in range(taps_x):
        partial_sum = jnp.dot(
            columns[shift_x : shift_x + rows_x].reshape(rows_x * rows_y, -1),
            banded[shift_x],
            preferred_element_type=jnp.float32,
        )
        output = partial_sum if output is None else output + partial_sum
    return output.reshape(rows_x, rows_y, -1)


def local(estimate, images, point_spread, covered):
    slab_x, width_y, depth = estimate.shape
    share_w = images.shape[2]
    view_count, taps_x, taps_y, taps_z = point_spread.shape
    rim_x, rim_y, rim_z = ((taps_x - 1) // 2, (taps_y - 1) // 2, (taps_z - 1) // 2)
    shares = width_y // share_w
    share_blocks = share_w // BY
    group = lax.axis_index("view")
    view_id = group // shares
    part = group % shares
    y_start = part * share_w
    source = estimate.astype(jnp.bfloat16)
    rimmed = with_halo(source, (("blk", 0),), rim_x)
    padded = jnp.pad(rimmed, ((0, 0), (rim_y, rim_y), (0, 0)))
    spread = lax.dynamic_index_in_dim(point_spread, view_id, 0, keepdims=False)
    kernel = (spread / jnp.sum(spread)).astype(jnp.bfloat16)
    forward = band_table(kernel, depth)
    backward = band_table(kernel[::-1, ::-1, ::-1], depth)
    coverage_row = lax.dynamic_index_in_dim(covered[:, 0, :], view_id, 0, keepdims=False) > 0
    share_cover = lax.dynamic_slice_in_dim(coverage_row, part * share_blocks, share_blocks)
    cell_cover = jnp.repeat(share_cover, BY)[None, :, None]
    image = images[0]
    region = lax.dynamic_slice(
        padded, (0, y_start, 0), (slab_x + 2 * rim_x, share_w + 2 * rim_y, depth)
    )
    blurred = convolve(region, forward, slab_x, share_w)
    quotient = jnp.where(cell_cover, image.astype(jnp.float32) / blurred, 0.0).astype(jnp.bfloat16)
    rim_zeros = jnp.zeros((slab_x, rim_y, depth), jnp.bfloat16)
    edge_rows = jnp.where(part == 0, quotient[:, share_w - rim_y :, :], quotient[:, :rim_y, :])
    partner = swapped(edge_rows, "view", 0)
    lower_rim = jnp.where(part > 0, partner, rim_zeros)
    upper_rim = jnp.where(part < shares - 1, partner, rim_zeros)
    extended = jnp.concatenate([lower_rim, quotient, upper_rim], axis=1)
    quotient_rimmed = with_halo(extended, (("blk", 0),), rim_x)
    correction = convolve(quotient_rimmed, backward, slab_x, share_w)
    share_factor = jnp.where(cell_cover, correction, 1.0)
    n_view = lax.axis_size("view")
    step_x = slab_x // n_view
    rows = share_factor.reshape(n_view, step_x, share_w, depth)
    got = lax.all_to_all(rows, "view", 0, 0)
    got = got.reshape(n_view // shares, shares, step_x, share_w, depth)
    product_rows = jnp.prod(got, axis=0)
    product_rows = jnp.transpose(product_rows, (1, 0, 2, 3)).reshape(step_x, width_y, depth)
    mine = lax.dynamic_slice_in_dim(estimate, group * step_x, step_x, axis=0)
    return lax.all_gather(mine * product_rows, "view", axis=0, tiled=True)


def solution(mesh):
    in_specs = (P("blk", None, None), P("view", "blk", None, None), P(), P(None, "blk", None))
    out_specs = P("blk", None, None)
    return jax.shard_map(local, mesh=mesh, in_specs=in_specs, out_specs=out_specs, check_vma=False)
```

profile of v0, /device:TPU:1, one launch (start us, length us, event | category | flops | bytes accessed | tf_op | source)
XLA Modules:
  0.0 128.2 jit_solution(17272270914108477657)
XLA Ops:
  6.5 1.3 %convert_element_type.30 = bf16[16,128,128]{2,1,0:T(8,128)(2,1)S(1)} convert(f32[16,128,128]{2,1,0:T(8,128)} %param.4) | non-fusion elementwise | flops 262144 | bytes 1572864 | tf_op jit(solution)/shard_map/convert_element_type | solution.py:91
  7.9 4.0 %collective-permute-start = (bf16[4,128,128]{2,1,0:T(8,128)(2,1)S(1)}, bf16[4,128,128]{2,1,0:T(8,128)(2,1)S(1)}, u32[]{:S(2)}, u32[]{:S(2)}) collective-permute-start(bf16[4,128,128]{2,1,0:T(8,128)(2,1)S(1)} %get-tuple-element.44), channel_id=1, source_target_pairs={{0,1},{1,2},{2,3},{3,4},{4,5},{5,6},{6,7},{7,8},{8,9},{9,10},{10,1... | collective-permute-start | bytes 393224 | tf_op jit(solution)/shard_map/ppermute | solution.py:17
  11.8 1.3 %collective-permute-start.1 = (bf16[4,128,128]{2,1,0:T(8,128)(2,1)S(1)}, bf16[4,128,128]{2,1,0:T(8,128)(2,1)S(1)}, u32[]{:S(2)}, u32[]{:S(2)}) collective-permute-start(bf16[4,128,128]{2,1,0:T(8,128)(2,1)S(1)} %get-tuple-element.43), channel_id=1, source_target_pairs={{1,0},{2,1},{3,2},{4,3},{5,4},{6,5},{7,6},{8,7},{9,8},{10,9},{11,1... | collective-permute-start | bytes 393224 | tf_op jit(solution)/shard_map/ppermute | solution.py:19
  13.2 1.6 %fusion.30 = (f32[]{:T(128)}, f32[1,9,7,25]{3,0,2,1:T(1,128)S(1)}) fusion(f32[8,9,7,25]{3,0,2,1:T(8,128)} %param.6, s32[]{:T(128)S(6)} %select_n.62), kind=kLoop, calls=%fused_computation.73 | loop fusion | flops 1574 | bytes 12608 | tf_op jit(solution)/shard_map/reduce_sum | solution.py:95
  14.8 1.5 %fusion.5 = bf16[9,7,128,128]{3,1,2,0:T(8,128)(2,1)S(1)} fusion(f32[1,9,7,25]{3,0,2,1:T(1,128)S(1)} %get-tuple-element.6, f32[]{:T(128)} %get-tuple-element.5), kind=kOutput, calls=%fused_computation.4 | convolution fusion | flops 53873744 | bytes 2070688 | tf_op jit(solution)/shard_map/abt,tpz->abpz/dot_general | solution.py:57
  17.6 0.7 fusion.29
  19.9 3.2 %fusion.32 = (bf16[16,64,896]{2,1,0:T(8,128)(2,1)S(1)}, bf16[16,64,896]{2,1,0:T(8,128)(2,1)S(1)}, bf16[16,64,896]{2,1,0:T(8,128)(2,1)S(1)}, bf16[16,64,896]{2,1,...) fusion(bf16[24,64,896]{2,1,0:T(8,128)(2,1)S(1)} %slice_dynamic-, ...), kind=kLoop, calls=%fused_computation.75 | loop fusion | bytes 33030144 | tf_op jit(solution)/shard_map/slice | solution.py:72
  23.8 0.7 convolution_add_fusion.15
  24.4 0.6 convolution_add_fusion.14
  25.7 0.6 convolution_add_fusion.12
  28.4 0.7 convolution_add_fusion.8
  29.5 1.3 %collective-permute-start.2 = (bf16[16,3,128]{2,1,0:T(4,128)(2,1)S(1)}, bf16[16,3,128]{2,1,0:T(4,128)(2,1)S(1)}, u32[]{:S(2)}, u32[]{:S(2)}) collective-permute-start(bf16[16,3,128]{2,1,0:T(4,128)(2,1)S(1)} %slice_select_fusion), channel_id=1, source_target_pairs={{0,16},{16,0},{32,48},{48,32},{64,80},{80,64},{96,112},{112,96},{1... | collective-permute-start | bytes 36872 | tf_op jit(solution)/shard_map/ppermute | solution.py:33
  30.8 0.9 fusion.8
  31.8 1.3 %collective-permute-start.4 = (bf16[4,70,128]{2,1,0:T(8,128)(2,1)S(1)}, bf16[4,70,128]{2,1,0:T(8,128)(2,1)S(1)}, u32[]{:S(2)}, u32[]{:S(2)}) collective-permute-start(bf16[4,70,128]{2,1,0:T(8,128)(2,1)S(1)} %get-tuple-element.46), channel_id=1, source_target_pairs={{1,0},{2,1},{3,2},{4,3},{5,4},{6,5},{7,6},{8,7},{9,8},{10,9},{11,1... | collective-permute-start | bytes 215048 | tf_op jit(solution)/shard_map/ppermute | solution.py:19
  33.1 4.8 %collective-permute-start.3 = (bf16[4,70,128]{2,1,0:T(8,128)(2,1)S(1)}, bf16[4,70,128]{2,1,0:T(8,128)(2,1)S(1)}, u32[]{:S(2)}, u32[]{:S(2)}) collective-permute-start(bf16[4,70,128]{2,1,0:T(8,128)(2,1)S(1)} %get-tuple-element.45), channel_id=1, source_target_pairs={{0,1},{1,2},{2,3},{3,4},{4,5},{5,6},{6,7},{7,8},{8,9},{9,10},{10,1... | collective-permute-start | bytes 215048 | tf_op jit(solution)/shard_map/ppermute | solution.py:17
  40.3 3.2 %fusion.31 = (bf16[16,64,896]{2,1,0:T(8,128)(2,1)S(1)}, bf16[16,64,896]{2,1,0:T(8,128)(2,1)S(1)}, bf16[16,64,896]{2,1,0:T(8,128)(2,1)S(1)}, bf16[16,64,896]{2,1,...) fusion(bf16[24,64,896]{2,1,0:T(8,128)(2,1)S(1)} %slice_dynamic-, ...), kind=kLoop, calls=%fused_computation.74 | loop fusion | bytes 33030144 | tf_op jit(solution)/shard_map/slice | solution.py:72
  44.2 0.7 convolution_add_fusion.7
  44.8 0.6 convolution_add_fusion.6
  49.4 0.9 broadcast_select_fusion
  50.3 9.6 %all-to-all-start = ((f32[16,1,64,128]{3,2,1,0:T(8,128)}), f32[16,1,64,128]{3,2,1,0:T(8,128)S(1)}, u32[]{:S(2)}, u32[]{:S(2)}) async-start(f32[16,1,64,128]{3,2,1,0:T(8,128)} %broadcast_select_fusion), calls=%async_computation | async-start | bytes 1048576 | tf_op jit(solution)/shard_map/all_to_all | solution.py:119
  60.0 17.3 %all-to-all-done = f32[16,1,64,128]{3,2,1,0:T(8,128)S(1)} async-done(((f32[16,1,64,128]{3,2,1,0:T(8,128)}), f32[16,1,64,128]{3,2,1,0:T(8,128)S(1)}, u32[]{:S(2)}, u32[]{:S(2)}) %all-to-all-start) | async-done | bytes 524320 | tf_op jit(solution)/shard_map/all_to_all | solution.py:119
  77.3 1.5 %bitcast_multiply_fusion = f32[1,128,128]{2,1,0:T(8,128)} fusion(f32[16,128,128]{2,1,0:T(8,128)} %param.4, s32[]{:T(128)S(6)} %select_n.60, f32[1,128,128]{2,1,0:T(8,128)S(1)} %bitcast.144), kind=kLoop, calls=%fused_computation.59 | loop fusion | flops 16384 | bytes 196612 | tf_op jit(solution)/shard_map/mul | solution.py:124
  78.8 40.3 %all-gather.2.cloned.1.call-done = f32[16,128,128]{2,1,0:T(8,128)} async-done(((f32[1,128,128]{2,1,0:T(8,128)}), f32[16,128,128]{2,1,0:T(8,128)}) %all-gather.2.cloned.1.call-update) | async-done | bytes 1048592 | tf_op jit(solution)/shard_map/all_gather | solution.py:124
  119.1 2.3 %copy.70 = f32[16,128,128]{2,1,0:T(8,128)} copy(f32[16,128,128]{2,1,0:T(8,128)} %all-gather.2.cloned.1.call-done) | data formatting | bytes 2097152
  (70 shorter events, 13.5 us)
Async XLA Ops:
  7.9 10.5 %collective-permute-start = (bf16[4,128,128]{2,1,0:T(8,128)(2,1)S(1)}, bf16[4,128,128]{2,1,0:T(8,128)(2,1)S(1)}, u32[]{:S(2)}, u32[]{:S(2)}) collective-permute-start(bf16[4,128,128]{2,1,0:T(8,128)(2,1)S(1)} %get-tuple-element.44), channel_id=1, source_target_pairs={{0,1},{1,2},{2,3},{3,4},{4,5},{5,6},{6,7},{7,8},{8,9},{9,10},{10,1... | collective-permute-start | bytes 393224 | tf_op jit(solution)/shard_map/ppermute | solution.py:17
  11.8 6.6 %collective-permute-start.1 = (bf16[4,128,128]{2,1,0:T(8,128)(2,1)S(1)}, bf16[4,128,128]{2,1,0:T(8,128)(2,1)S(1)}, u32[]{:S(2)}, u32[]{:S(2)}) collective-permute-start(bf16[4,128,128]{2,1,0:T(8,128)(2,1)S(1)} %get-tuple-element.43), channel_id=1, source_target_pairs={{1,0},{2,1},{3,2},{4,3},{5,4},{6,5},{7,6},{8,7},{9,8},{10,9},{11,1... | collective-permute-start | bytes 393224 | tf_op jit(solution)/shard_map/ppermute | solution.py:19
  16.6 0.7 copy-start.1
  28.3 1.0 copy-start
  29.5 2.2 %collective-permute-start.2 = (bf16[16,3,128]{2,1,0:T(4,128)(2,1)S(1)}, bf16[16,3,128]{2,1,0:T(4,128)(2,1)S(1)}, u32[]{:S(2)}, u32[]{:S(2)}) collective-permute-start(bf16[16,3,128]{2,1,0:T(4,128)(2,1)S(1)} %slice_select_fusion), channel_id=1, source_target_pairs={{0,16},{16,0},{32,48},{48,32},{64,80},{80,64},{96,112},{112,96},{1... | collective-permute-start | bytes 36872 | tf_op jit(solution)/shard_map/ppermute | solution.py:33
  31.8 6.7 %collective-permute-start.4 = (bf16[4,70,128]{2,1,0:T(8,128)(2,1)S(1)}, bf16[4,70,128]{2,1,0:T(8,128)(2,1)S(1)}, u32[]{:S(2)}, u32[]{:S(2)}) collective-permute-start(bf16[4,70,128]{2,1,0:T(8,128)(2,1)S(1)} %get-tuple-element.46), channel_id=1, source_target_pairs={{1,0},{2,1},{3,2},{4,3},{5,4},{6,5},{7,6},{8,7},{9,8},{10,9},{11,1... | collective-permute-start | bytes 215048 | tf_op jit(solution)/shard_map/ppermute | solution.py:19
  33.1 6.0 %collective-permute-start.3 = (bf16[4,70,128]{2,1,0:T(8,128)(2,1)S(1)}, bf16[4,70,128]{2,1,0:T(8,128)(2,1)S(1)}, u32[]{:S(2)}, u32[]{:S(2)}) collective-permute-start(bf16[4,70,128]{2,1,0:T(8,128)(2,1)S(1)} %get-tuple-element.45), channel_id=1, source_target_pairs={{0,1},{1,2},{2,3},{3,4},{4,5},{5,6},{6,7},{7,8},{8,9},{9,10},{10,1... | collective-permute-start | bytes 215048 | tf_op jit(solution)/shard_map/ppermute | solution.py:17
  50.3 26.9 %all-to-all-start = ((f32[16,1,64,128]{3,2,1,0:T(8,128)}), f32[16,1,64,128]{3,2,1,0:T(8,128)S(1)}, u32[]{:S(2)}, u32[]{:S(2)}) async-start(f32[16,1,64,128]{3,2,1,0:T(8,128)} %broadcast_select_fusion), calls=%async_computation | async-start | bytes 1048576 | tf_op jit(solution)/shard_map/all_to_all | solution.py:119
  60.0 59.1 %all-gather.2.cloned.1.call-start = ((), (), s32[]{:S(2)}) async-start(), calls=%async_computation.1 | async-start | bytes 1114112 | tf_op jit(solution)/shard_map/all_gather | solution.py:124
Sparse Core Ops, SparseCore 0:
  78.9 40.0 all-gather.1
where the time goes:
time: 129 us; the launch traced here: 128 us
  waiting for transfers between devices  58.2 us (45%)
  starting transfers between devices  22.3 us (17%)
  matrix products  14 us (11%)
  between operations  14 us (11%)
  local copies, waits for them, and re-layouts  12.9 us (10%)
  other arithmetic  6.78 us (5%)
    all_gather x1, waiting for transfers between devices, local(): return lax.all_gather(mine * product_rows, 'view', axis=0, tiled=True)  40.3 us
    all_to_all x1, waiting for transfers between devices, local(): got = lax.all_to_all(rows, 'view', 0, 0)  17.3 us
    dot_general x18, matrix products, convolve(): jnp.dot(columns[shift_x:shift_x + rows_x].reshape(rows_x * rows_y, -1), b...  11.7 us
    all_to_all x1, starting transfers between devices, local(): got = lax.all_to_all(rows, 'view', 0, 0)  9.63 us
    ppermute x2, starting transfers between devices, with_halo(): lax.ppermute(tail, axis, [(i, (i + 1) % count) for i in range(ends)])  8.75 us
    slice x2, local copies, waits for them, and re-layouts, convolve(): columns[shift_x:shift_x + rows_x].reshape(rows_x * rows_y, -1)  6.38 us
    unnamed x17, local copies, waits for them, and re-layouts  4.82 us
    ppermute x2, starting transfers between devices, with_halo(): lax.ppermute(head, axis, [((i + 1) % count, i) for i in range(ends)])  2.58 us
  transfers between devices with their start and end apart: 7, of which 3 were waited for; matrix products, arithmetic and copies ran while one was open for 5% of the time, Pallas kernels for 0%

commit v1 on v0

--- a/solution.py
+++ b/solution.py
@@ -4,6 +4,11 @@
 from jax.sharding import PartitionSpec as P
 
 BY = 32
+
+
+def gather_from_all(x, axis, dim):
+    copies = jnp.concatenate([x] * lax.axis_size(axis), axis=dim)
+    return lax.all_to_all(copies, axis, dim, dim, tiled=True)
 
 
 def with_halo(cells, sides, width):
@@ -121,7 +126,7 @@
     product_rows = jnp.prod(got, axis=0)
     product_rows = jnp.transpose(product_rows, (1, 0, 2, 3)).reshape(step_x, width_y, depth)
     mine = lax.dynamic_slice_in_dim(estimate, group * step_x, step_x, axis=0)
-    return lax.all_gather(mine * product_rows, "view", axis=0, tiled=True)
+    return gather_from_all(mine * product_rows, "view", 0)
 
 
 def solution(mesh):

time: 129 us -> 110 us (0.85)
  the two profiles are of different devices: /device:TPU:1 before, /device:TPU:25 now
where the time goes in v1:
time: 110 us
  blocking collectives  31.3 us (28%)
  starting transfers between devices  24.4 us (22%)
  waiting for transfers between devices  21.9 us (20%)
  matrix products  14 us (13%)
  local copies, waits for them, and re-layouts  11.7 us (11%)
  other arithmetic  6.15 us (6%)
    all_to_all x1, blocking collectives, gather_from_all(): return lax.all_to_all(copies, axis, dim, dim, tiled=True)  31.3 us
    all_to_all x1, waiting for transfers between devices, local(): got = lax.all_to_all(rows, 'view', 0, 0)  17.3 us
    dot_general x18, matrix products, convolve(): jnp.dot(columns[shift_x:shift_x + rows_x].reshape(rows_x * rows_y, -1), b...  11.6 us
    all_to_all x1, starting transfers between devices, local(): got = lax.all_to_all(rows, 'view', 0, 0)  10.2 us
    ppermute x2, starting transfers between devices, with_halo(): lax.ppermute(head, axis, [((i + 1) % count, i) for i in range(ends)])  7.67 us
    slice x2, local copies, waits for them, and re-layouts, convolve(): columns[shift_x:shift_x + rows_x].reshape(rows_x * rows_y, -1)  6.38 us
    ppermute x2, starting transfers between devices, with_halo(): lax.ppermute(tail, axis, [(i, (i + 1) % count) for i in range(ends)])  5.22 us
    ppermute x2, waiting for transfers between devices, with_halo(): lax.ppermute(tail, axis, [(i, (i + 1) % count) for i in range(ends)])  4.54 us
  transfers between devices with their start and end apart: 6, of which 2 were waited for; matrix products, arithmetic and copies ran while one was open for 6% of the time, Pallas kernels for 0%

profile of v1, /device:TPU:25, one launch (start us, length us, event | category | flops | bytes accessed | tf_op | source)
XLA Modules:
  0.0 110.0 jit_solution(11583578486269500536)
XLA Ops:
  0.0 1.3 %convert_element_type.30 = bf16[16,128,128]{2,1,0:T(8,128)(2,1)S(1)} convert(f32[16,128,128]{2,1,0:T(8,128)} %param.4) | non-fusion elementwise | flops 262144 | bytes 1572864 | tf_op jit(solution)/shard_map/convert_element_type | solution.py:96
  1.3 3.1 %collective-permute-start = (bf16[4,128,128]{2,1,0:T(8,128)(2,1)S(1)}, bf16[4,128,128]{2,1,0:T(8,128)(2,1)S(1)}, u32[]{:S(2)}, u32[]{:S(2)}) collective-permute-start(bf16[4,128,128]{2,1,0:T(8,128)(2,1)S(1)} %get-tuple-element.44), channel_id=1, source_target_pairs={{0,1},{1,2},{2,3},{3,4},{4,5},{5,6},{6,7},{7,8},{8,9},{9,10},{10,1... | collective-permute-start | bytes 393224 | tf_op jit(solution)/shard_map/ppermute | solution.py:22
  4.5 4.3 %collective-permute-start.1 = (bf16[4,128,128]{2,1,0:T(8,128)(2,1)S(1)}, bf16[4,128,128]{2,1,0:T(8,128)(2,1)S(1)}, u32[]{:S(2)}, u32[]{:S(2)}) collective-permute-start(bf16[4,128,128]{2,1,0:T(8,128)(2,1)S(1)} %get-tuple-element.43), channel_id=1, source_target_pairs={{1,0},{2,1},{3,2},{4,3},{5,4},{6,5},{7,6},{8,7},{9,8},{10,9},{11,1... | collective-permute-start | bytes 393224 | tf_op jit(solution)/shard_map/ppermute | solution.py:24
  8.8 1.6 %fusion.31 = (f32[]{:T(128)}, f32[1,9,7,25]{3,0,2,1:T(1,128)S(1)}) fusion(f32[8,9,7,25]{3,0,2,1:T(8,128)} %param.6, s32[]{:T(128)S(6)} %select_n.62), kind=kLoop, calls=%fused_computation.74 | loop fusion | flops 1574 | bytes 12608 | tf_op jit(solution)/shard_map/reduce_sum | solution.py:100
  10.4 1.5 %fusion.5 = bf16[9,7,128,128]{3,1,2,0:T(8,128)(2,1)S(1)} fusion(f32[1,9,7,25]{3,0,2,1:T(1,128)S(1)} %get-tuple-element.6, f32[]{:T(128)} %get-tuple-element.5), kind=kOutput, calls=%fused_computation.4 | convolution fusion | flops 53873744 | bytes 2070688 | tf_op jit(solution)/shard_map/abt,tpz->abpz/dot_general | solution.py:62
  13.2 0.7 fusion.30
  15.5 3.2 %fusion.33 = (bf16[16,64,896]{2,1,0:T(8,128)(2,1)S(1)}, bf16[16,64,896]{2,1,0:T(8,128)(2,1)S(1)}, bf16[16,64,896]{2,1,0:T(8,128)(2,1)S(1)}, bf16[16,64,896]{2,1,...) fusion(bf16[24,64,896]{2,1,0:T(8,128)(2,1)S(1)} %slice_dynamic-, ...), kind=kLoop, calls=%fused_computation.76 | loop fusion | bytes 33030144 | tf_op jit(solution)/shard_map/slice | solution.py:77
  20.0 0.6 convolution_add_fusion.14
  20.7 0.6 convolution_add_fusion.13
  22.0 0.6 convolution_add_fusion.11
  22.6 0.6 convolution_add_fusion.10
  24.0 0.7 convolution_add_fusion.8
  25.1 1.3 %collective-permute-start.2 = (bf16[16,3,128]{2,1,0:T(4,128)(2,1)S(1)}, bf16[16,3,128]{2,1,0:T(4,128)(2,1)S(1)}, u32[]{:S(2)}, u32[]{:S(2)}) collective-permute-start(bf16[16,3,128]{2,1,0:T(4,128)(2,1)S(1)} %slice_select_fusion), channel_id=1, source_target_pairs={{0,16},{16,0},{32,48},{48,32},{64,80},{80,64},{96,112},{112,96},{1... | collective-permute-start | bytes 36872 | tf_op jit(solution)/shard_map/ppermute | solution.py:38
  26.4 0.9 fusion.8
  27.4 3.4 %collective-permute-start.4 = (bf16[4,70,128]{2,1,0:T(8,128)(2,1)S(1)}, bf16[4,70,128]{2,1,0:T(8,128)(2,1)S(1)}, u32[]{:S(2)}, u32[]{:S(2)}) collective-permute-start(bf16[4,70,128]{2,1,0:T(8,128)(2,1)S(1)} %get-tuple-element.46), channel_id=1, source_target_pairs={{1,0},{2,1},{3,2},{4,3},{5,4},{6,5},{7,6},{8,7},{9,8},{10,9},{11,1... | collective-permute-start | bytes 215048 | tf_op jit(solution)/shard_map/ppermute | solution.py:24
  30.8 2.1 %collective-permute-start.3 = (bf16[4,70,128]{2,1,0:T(8,128)(2,1)S(1)}, bf16[4,70,128]{2,1,0:T(8,128)(2,1)S(1)}, u32[]{:S(2)}, u32[]{:S(2)}) collective-permute-start(bf16[4,70,128]{2,1,0:T(8,128)(2,1)S(1)} %get-tuple-element.45), channel_id=1, source_target_pairs={{0,1},{1,2},{2,3},{3,4},{4,5},{5,6},{6,7},{7,8},{8,9},{9,10},{10,1... | collective-permute-start | bytes 215048 | tf_op jit(solution)/shard_map/ppermute | solution.py:22
  33.5 4.5 %collective-permute-done.3 = bf16[4,70,128]{2,1,0:T(8,128)(2,1)S(1)} collective-permute-done((bf16[4,70,128]{2,1,0:T(8,128)(2,1)S(1)}, bf16[4,70,128]{2,1,0:T(8,128)(2,1)S(1)}, u32[]{:S(2)}, u32[]{:S(2)}) %collective-permute-start.3) | collective-permute-done | bytes 71712 | tf_op jit(solution)/shard_map/ppermute | solution.py:22
  39.3 3.2 %fusion.32 = (bf16[16,64,896]{2,1,0:T(8,128)(2,1)S(1)}, bf16[16,64,896]{2,1,0:T(8,128)(2,1)S(1)}, bf16[16,64,896]{2,1,0:T(8,128)(2,1)S(1)}, bf16[16,64,896]{2,1,...) fusion(bf16[24,64,896]{2,1,0:T(8,128)(2,1)S(1)} %slice_dynamic-, ...), kind=kLoop, calls=%fused_computation.75 | loop fusion | bytes 33030144 | tf_op jit(solution)/shard_map/slice | solution.py:77
  48.3 0.9 broadcast_select_fusion
  49.2 10.2 %all-to-all-start = ((f32[16,1,64,128]{3,2,1,0:T(8,128)}), f32[16,1,64,128]{3,2,1,0:T(8,128)S(1)}, u32[]{:S(2)}, u32[]{:S(2)}) async-start(f32[16,1,64,128]{3,2,1,0:T(8,128)} %broadcast_select_fusion), calls=%async_computation | async-start | bytes 1048576 | tf_op jit(solution)/shard_map/all_to_all | solution.py:124
  59.4 17.3 %all-to-all-done = f32[16,1,64,128]{3,2,1,0:T(8,128)S(1)} async-done(((f32[16,1,64,128]{3,2,1,0:T(8,128)}), f32[16,1,64,128]{3,2,1,0:T(8,128)S(1)}, u32[]{:S(2)}, u32[]{:S(2)}) %all-to-all-start) | async-done | bytes 524320 | tf_op jit(solution)/shard_map/all_to_all | solution.py:124
  76.8 0.9 fusion.23
  77.7 31.3 %all_to_all.10 = f32[16,128,128]{2,1,0:T(8,128)S(1)} all-to-all(f32[16,128,128]{2,1,0:T(8,128)S(1)} %concatenate.23), channel_id=1, replica_groups=mesh['view'=16,'blk'=16] {'view'}, dimensions={0} | all-to-all | bytes 2097152 | tf_op jit(solution)/shard_map/all_to_all | solution.py:11
  109.0 1.0 copy.70
  (69 shorter events, 13.5 us)
Async XLA Ops:
  1.3 12.7 %collective-permute-start = (bf16[4,128,128]{2,1,0:T(8,128)(2,1)S(1)}, bf16[4,128,128]{2,1,0:T(8,128)(2,1)S(1)}, u32[]{:S(2)}, u32[]{:S(2)}) collective-permute-start(bf16[4,128,128]{2,1,0:T(8,128)(2,1)S(1)} %get-tuple-element.44), channel_id=1, source_target_pairs={{0,1},{1,2},{2,3},{3,4},{4,5},{5,6},{6,7},{7,8},{8,9},{9,10},{10,1... | collective-permute-start | bytes 393224 | tf_op jit(solution)/shard_map/ppermute | solution.py:22
  4.5 9.6 %collective-permute-start.1 = (bf16[4,128,128]{2,1,0:T(8,128)(2,1)S(1)}, bf16[4,128,128]{2,1,0:T(8,128)(2,1)S(1)}, u32[]{:S(2)}, u32[]{:S(2)}) collective-permute-start(bf16[4,128,128]{2,1,0:T(8,128)(2,1)S(1)} %get-tuple-element.43), channel_id=1, source_target_pairs={{1,0},{2,1},{3,2},{4,3},{5,4},{6,5},{7,6},{8,7},{9,8},{10,9},{11,1... | collective-permute-start | bytes 393224 | tf_op jit(solution)/shard_map/ppermute | solution.py:24
  12.2 0.7 copy-start.1
  24.0 1.0 copy-start
  25.1 2.2 %collective-permute-start.2 = (bf16[16,3,128]{2,1,0:T(4,128)(2,1)S(1)}, bf16[16,3,128]{2,1,0:T(4,128)(2,1)S(1)}, u32[]{:S(2)}, u32[]{:S(2)}) collective-permute-start(bf16[16,3,128]{2,1,0:T(4,128)(2,1)S(1)} %slice_select_fusion), channel_id=1, source_target_pairs={{0,16},{16,0},{32,48},{48,32},{64,80},{80,64},{96,112},{112,96},{1... | collective-permute-start | bytes 36872 | tf_op jit(solution)/shard_map/ppermute | solution.py:38
  27.4 6.1 %collective-permute-start.4 = (bf16[4,70,128]{2,1,0:T(8,128)(2,1)S(1)}, bf16[4,70,128]{2,1,0:T(8,128)(2,1)S(1)}, u32[]{:S(2)}, u32[]{:S(2)}) collective-permute-start(bf16[4,70,128]{2,1,0:T(8,128)(2,1)S(1)} %get-tuple-element.46), channel_id=1, source_target_pairs={{1,0},{2,1},{3,2},{4,3},{5,4},{6,5},{7,6},{8,7},{9,8},{10,9},{11,1... | collective-permute-start | bytes 215048 | tf_op jit(solution)/shard_map/ppermute | solution.py:24
  30.8 7.2 %collective-permute-start.3 = (bf16[4,70,128]{2,1,0:T(8,128)(2,1)S(1)}, bf16[4,70,128]{2,1,0:T(8,128)(2,1)S(1)}, u32[]{:S(2)}, u32[]{:S(2)}) collective-permute-start(bf16[4,70,128]{2,1,0:T(8,128)(2,1)S(1)} %get-tuple-element.45), channel_id=1, source_target_pairs={{0,1},{1,2},{2,3},{3,4},{4,5},{5,6},{6,7},{7,8},{8,9},{9,10},{10,1... | collective-permute-start | bytes 215048 | tf_op jit(solution)/shard_map/ppermute | solution.py:22
  49.2 27.5 %all-to-all-start = ((f32[16,1,64,128]{3,2,1,0:T(8,128)}), f32[16,1,64,128]{3,2,1,0:T(8,128)S(1)}, u32[]{:S(2)}, u32[]{:S(2)}) async-start(f32[16,1,64,128]{3,2,1,0:T(8,128)} %broadcast_select_fusion), calls=%async_computation | async-start | bytes 1048576 | tf_op jit(solution)/shard_map/all_to_all | solution.py:124
